TPU v7x, 32 devices: a whole 2x2x4 slice. The times are simulated.
32 devices in a mesh: grp: 2 (over core), cores: 16 (over z, y, x).
Axes of the slice: x: 2, y: 2, z: 4, core: 2. Of those that a mesh axis runs over, the one named last changes fastest.
Arguments:
- rhs_core: float32 [4, 8192], P(None, 'cores'), may hold values from -6 to 6
- rhs_noncore: float32 [4, 8192], P(None, ('grp', 'cores')), may hold values from -6 to 6
- records_core: float32 [4, 8192], P(None, 'cores'), may hold values from 0.2 to 2
- records_noncore: float32 [4, 8192], P(None, ('grp', 'cores')), may hold values from 0.2 to 2
- core_inverse: bfloat16 [8192, 8192], P('cores'), as said below
- genomic_block: bfloat16 [8192, 8192], P(('grp', 'cores')), may hold values from -0.125 to 0.125
- m_inverse: float32 [8192], P(('grp', 'cores')), may hold values from 0.5 to 4
- trait_inverse: float32 [4, 4], replicated, as said below
Outputs:
- sol_core: float32 [4, 8192], P(None, 'cores')
- sol_noncore: float32 [4, 8192], P(None, ('grp', 'cores'))
- res_core: float32 [4, 8192], P(None, 'cores')
- res_noncore: float32 [4, 8192], P(None, ('grp', 'cores'))
Inputs may be any that keep to these rules, and one draw needn't show every extreme that they name: core_inverse is symmetric and positive definite. trait_inverse is symmetric and positive definite.
All inputs are finite; a program needn't handle non-finite values.
Results may differ from a plain program's by a relative error of at most 0.028.
Values may be sent and summed in bfloat16 or wider, within the bound.
No kernel may reach another device: no remote copies, remote signals or barrier semaphores. Data moves between devices by JAX's collectives and lax.ppermute only.
A program may use at most 64 MiB of HBM per device.

v0:
```python
import jax
import jax.numpy as jnp
from jax import lax
from jax.sharding import PartitionSpec as P

ITERS = 2


def genomic_map(core_vec, non_vec, core_inverse, genomic_block, m_inverse):
    core_in = core_vec.astype(jnp.bfloat16)
    partial_map = jnp.dot(core_in, core_inverse, preferred_element_type=jnp.float32)
    mapped = lax.psum(partial_map, "cores")
    mapped_in = mapped.astype(jnp.bfloat16)
    pulled = lax.dot_general(
        mapped_in, genomic_block, (((1,), (1,)), ((), ())), preferred_element_type=jnp.float32
    )
    scaled = m_inverse[None, :] * (non_vec - pulled)
    pushed_part = jnp.dot(
        scaled.astype(jnp.bfloat16), genomic_block, preferred_element_type=jnp.float32
    )
    grouped = lax.psum(pushed_part.astype(jnp.bfloat16), "grp")
    pushed = lax.psum_scatter(grouped, "cores", scatter_dimension=1, tiled=True).astype(jnp.float32)
    remainder = (core_vec - pushed).astype(jnp.bfloat16)
    back_part = jnp.dot(remainder, core_inverse, preferred_element_type=jnp.float32)
    core_out = lax.psum_scatter(
        back_part.astype(jnp.bfloat16), "cores", scatter_dimension=1, tiled=True
    ).astype(jnp.float32)
    return (core_out, scaled)


def body(
    rhs_core,
    rhs_noncore,
    records_core,
    records_noncore,
    core_inverse,
    genomic_block,
    m_inverse,
    trait_inverse,
):
    highest = lax.Precision.HIGHEST
    first_copy = (lax.axis_index("grp") == 0).astype(jnp.float32)
    trait_diag = jnp.diagonal(trait_inverse)[:, None]
    prec_core = 1.0 / (records_core + trait_diag)
    prec_non = 1.0 / (records_noncore + trait_diag * m_inverse[None, :])
    sol_core = jnp.zeros_like(rhs_core)
    sol_non = jnp.zeros_like(rhs_noncore)
    res_core, res_non = (rhs_core, rhs_noncore)
    z_core, z_non = (prec_core * res_core, prec_non * res_non)
    dir_core, dir_non = (z_core, z_non)

    def residual_inner(core_a, core_b, non_a, non_b):
        local_sum = jnp.sum(non_a * non_b) + first_copy * jnp.sum(core_a * core_b)
        return lax.psum(local_sum, ("grp", "cores"))

    rz_now = residual_inner(res_core, z_core, res_non, z_non)
    for iteration in range(ITERS):
        core_out, non_out = genomic_map(dir_core, dir_non, core_inverse, genomic_block, m_inverse)
        image_core = records_core * dir_core + jnp.dot(trait_inverse, core_out, precision=highest)
        image_non = records_noncore * dir_non + jnp.dot(trait_inverse, non_out, precision=highest)
        local_curve = jnp.sum(dir_non * image_non) + first_copy * jnp.sum(dir_core * image_core)
        step_size = rz_now / lax.psum(local_curve, ("grp", "cores"))
        sol_core = sol_core + step_size * dir_core
        sol_non = sol_non + step_size * dir_non
        res_core = res_core - step_size * image_core
        res_non = res_non - step_size * image_non
        if iteration + 1 < ITERS:
            z_core, z_non = (prec_core * res_core, prec_non * res_non)
            rz_next = residual_inner(res_core, z_core, res_non, z_non)
            factor = rz_next / rz_now
            dir_core = z_core + factor * dir_core
            dir_non = z_non + factor * dir_non
            rz_now = rz_next
    return (sol_core, sol_non, res_core, res_non)


def solution(mesh):
    in_specs = (
        P(None, "cores"),
        P(None, ("grp", "cores")),
        P(None, "cores"),
        P(None, ("grp", "cores")),
        P("cores", None),
        P(("grp", "cores"), None),
        P(("grp", "cores")),
        P(),
    )
    out_specs = (
        P(None, "cores"),
        P(None, ("grp", "cores")),
        P(None, "cores"),
        P(None, ("grp", "cores")),
    )
    return jax.shard_map(body, mesh=mesh, in_specs=in_specs, out_specs=out_specs, check_vma=False)
```

profile of v0, /device:TPU:12, one launch (start us, length us, event | category | flops | bytes accessed | tf_op | source)
XLA Modules:
  0.0 657.4 jit_solution(4603464972572962994)
XLA Ops:
  9.3 4.6 fusion.12
  13.9 67.9 %all-reduce.3 = bf16[4,8192]{1,0:T(4,128)(2,1)S(1)} all-reduce(f32[4,8192]{1,0:T(4,128)S(1)} %fusion.12), channel_id=1, replica_groups=mesh['grp'=2,'cores'=16] {'cores'}, use_global_device_ids=true, to_apply=%region_3.4 | all-reduce | flops 32768 | bytes 196608 | tf_op jit(solution)/shard_map/psum | solution.py:12
  81.9 3.5 fusion.5
  86.1 1.9 copy.16
  88.1 78.8 %reduce-scatter.17.cloned.1.call-done = bf16[512,4]{1,0:T(8,128)(2,1)} async-done(((bf16[8192,4]{1,0:T(8,128)(2,1)}), bf16[512,4]{1,0:T(8,128)(2,1)}) %reduce-scatter.17.cloned.1.call-update) | async-done | bytes 4112
  166.9 1.0 copy.17
  167.9 2.5 psum.64
  170.4 4.6 convolution_convert_fusion.2
  174.9 1.9 copy.12
  177.7 77.5 %reduce-scatter.13.cloned.1.call-done = bf16[512,4]{1,0:T(8,128)(2,1)} async-done(((bf16[8192,4]{1,0:T(8,128)(2,1)}), bf16[512,4]{1,0:T(8,128)(2,1)}) %reduce-scatter.13.cloned.1.call-update) | async-done | bytes 4112
  255.2 1.7 multiply_reduce_fusion.2
  259.5 48.3 %all-reduce = (f32[]{:T(128)}, f32[]{:T(128)}) all-reduce(f32[]{:T(128)S(6)} %add.78, f32[]{:T(128)S(6)} %add.81), channel_id=1, replica_groups=mesh['grp'=2,'cores'=16] {'grp','cores'}, use_global_device_ids=true, to_apply=%region_2.3 | all-reduce | flops 2 | bytes 16 | tf_op jit(solution)/shard_map/psum | solution.py:54
  311.8 38.3 %psum.60 = f32[]{:T(128)} all-reduce(f32[]{:T(128)S(6)} %add.82), channel_id=1, replica_groups=mesh['grp'=2,'cores'=16] {'grp','cores'}, use_global_device_ids=true, to_apply=%region_12.13 | all-reduce | flops 1 | bytes 8 | tf_op jit(solution)/shard_map/psum | solution.py:54
  351.5 4.6 fusion.10
  356.1 67.8 %all-reduce.4 = bf16[4,8192]{1,0:T(4,128)(2,1)S(1)} all-reduce(f32[4,8192]{1,0:T(4,128)S(1)} %fusion.10), channel_id=1, replica_groups=mesh['grp'=2,'cores'=16] {'cores'}, use_global_device_ids=true, to_apply=%region_13.14 | all-reduce | flops 32768 | bytes 196608 | tf_op jit(solution)/shard_map/psum | solution.py:12
  423.9 3.5 fusion.3
  428.1 1.9 copy.18
  430.1 78.8 %reduce-scatter.19.cloned.1.call-done = bf16[512,4]{1,0:T(8,128)(2,1)} async-done(((bf16[8192,4]{1,0:T(8,128)(2,1)}), bf16[512,4]{1,0:T(8,128)(2,1)}) %reduce-scatter.19.cloned.1.call-update) | async-done | bytes 4112
  509.8 2.5 psum.65
  512.3 4.6 convolution_convert_fusion
  516.9 1.9 copy.14
  519.5 77.7 %reduce-scatter.15.cloned.1.call-done = bf16[512,4]{1,0:T(8,128)(2,1)} async-done(((bf16[8192,4]{1,0:T(8,128)(2,1)}), bf16[512,4]{1,0:T(8,128)(2,1)}) %reduce-scatter.15.cloned.1.call-update) | async-done | bytes 4112
  597.2 1.7 multiply_reduce_fusion
  600.2 48.1 %psum.63 = f32[]{:T(128)} all-reduce(f32[]{:T(128)S(6)} %add.87), channel_id=1, replica_groups=mesh['grp'=2,'cores'=16] {'grp','cores'}, use_global_device_ids=true, to_apply=%region_19.20 | all-reduce | flops 1 | bytes 8 | tf_op jit(solution)/shard_map/psum | solution.py:62
  (39 shorter events, 8.9 us)
Async XLA Ops:
  7.2 0.7 copy-start
  7.2 159.7 %reduce-scatter.17.cloned.1.call-start = ((), (), s32[]{:S(2)}) async-start(), calls=%async_computation.6 | async-start | bytes 2228224
  9.3 72.5 %copy-start.5 = (f32[4,256]{1,0:T(4,128)S(1)}, f32[4,256]{1,0:T(4,128)}, u32[]{:S(2)}) copy-start(f32[4,256]{1,0:T(4,128)} %param.11) | copy-start | bytes 12292
  9.3 72.5 %copy-start.6 = (f32[4,256]{1,0:T(4,128)S(1)}, f32[4,256]{1,0:T(4,128)}, u32[]{:S(2)}) copy-start(f32[4,256]{1,0:T(4,128)} %param.9) | copy-start | bytes 12292
  9.3 72.5 %copy-start.7 = (f32[256]{0:T(256)S(1)}, f32[256]{0:T(256)}, u32[]{:S(2)}) copy-start(f32[256]{0:T(256)} %param.14) | copy-start | bytes 3076
  81.8 3.6 copy-start.1
  88.0 167.1 %reduce-scatter.13.cloned.1.call-start = ((), (), s32[]{:S(2)}) async-start(), calls=%async_computation.4 | async-start | bytes 2228224
  174.9 80.2 %copy-start.3 = (f32[4,512]{1,0:T(4,128)S(1)}, f32[4,512]{1,0:T(4,128)}, u32[]{:S(2)}) copy-start(f32[4,512]{1,0:T(4,128)} %param.10) | copy-start | bytes 24580
  174.9 80.2 %copy-start.4 = (f32[4,512]{1,0:T(4,128)S(1)}, f32[4,512]{1,0:T(4,128)}, u32[]{:S(2)}) copy-start(f32[4,512]{1,0:T(4,128)} %param.8) | copy-start | bytes 24580
  176.9 332.0 %reduce-scatter.19.cloned.1.call-start = ((), (), s32[]{:S(2)}) async-start(), calls=%async_computation.7 | async-start | bytes 2228224
  423.9 3.5 copy-start.2
  430.0 167.2 %reduce-scatter.15.cloned.1.call-start = ((), (), s32[]{:S(2)}) async-start(), calls=%async_computation.5 | async-start | bytes 2228224
Sparse Core Ops, SparseCore 0:
  88.2 78.6 reduce-scatter.16
  177.0 78.1 reduce-scatter.12
  430.1 78.6 reduce-scatter.18
  518.9 78.2 reduce-scatter.14
where the time goes:
time: 658 us; the launch traced here: 657 us
  waiting for transfers between devices  313 us (48%)
  blocking collectives  275 us (42%)
  matrix products  31.7 us (5%)
  between operations  23.1 us (4%)
  local copies, waits for them, and re-layouts  10.9 us (2%)
    unnamed x8, waiting for transfers between devices  313 us
    psum x2, blocking collectives, genomic_map(): mapped = lax.psum(partial_map, 'cores')  136 us
    psum x2, blocking collectives, residual_inner(): return lax.psum(local_sum, ('grp', 'cores'))  86.5 us
    psum x1, blocking collectives, body(): step_size = rz_now / lax.psum(local_curve, ('grp', 'cores'))  48.1 us
  transfers between devices with their start and end apart: 4, of which 4 were waited for; matrix products, arithmetic and copies ran while one was open for 0% of the time, Pallas kernels for 0%

commit v1 on v0

--- a/solution.py
+++ b/solution.py
@@ -9,7 +9,7 @@
 def genomic_map(core_vec, non_vec, core_inverse, genomic_block, m_inverse):
     core_in = core_vec.astype(jnp.bfloat16)
     partial_map = jnp.dot(core_in, core_inverse, preferred_element_type=jnp.float32)
-    mapped = lax.psum(partial_map, "cores")
+    mapped = jnp.sum(lax.all_gather(partial_map, "cores"), axis=0)
     mapped_in = mapped.astype(jnp.bfloat16)
     pulled = lax.dot_general(
         mapped_in, genomic_block, (((1,), (1,)), ((), ())), preferred_element_type=jnp.float32

time: 658 us -> 637 us (0.968)
  blocking collectives: 275 us -> 140 us
  waiting for transfers between devices: 313 us -> 421 us
    psum x2 -> x0, blocking collectives: 136 us -> none  [genomic_map(): mapped = lax.psum(partial_map, 'cores')]
    all_gather x0 -> x2, waiting for transfers between devices: none -> 123 us  [genomic_map(): mapped = jnp.sum(lax.all_gather(partial_map, 'cores'), axis=0)]
    unnamed x8 -> x10, waiting for transfers between devices: 313 us -> 298 us
  transfers between devices with their start and end apart: 4 -> 6, of which waited for: 4 -> 6; matrix products, arithmetic and copies ran while one was open for 0% -> 0% of each run, Pallas kernels for 0% -> 0%
where the time goes in v1:
time: 637 us; the launch traced here: 636 us
  waiting for transfers between devices  421 us (66%)
  blocking collectives  140 us (22%)
  matrix products  33 us (5%)
  between operations  23.4 us (4%)
  local copies, waits for them, and re-layouts  10.9 us (2%)
  other arithmetic  7.38 us (1%)
    unnamed x10, waiting for transfers between devices  298 us
    all_gather x2, waiting for transfers between devices, genomic_map(): mapped = jnp.sum(lax.all_gather(partial_map, 'cores'), axis=0)  123 us
    psum x2, blocking collectives, residual_inner(): return lax.psum(local_sum, ('grp', 'cores'))  86.5 us
    psum x1, blocking collectives, body(): step_size = rz_now / lax.psum(local_curve, ('grp', 'cores'))  48.3 us
  transfers between devices with their start and end apart: 6, of which 6 were waited for; matrix products, arithmetic and copies ran while one was open for 0% of the time, Pallas kernels for 0%

profile of v1, /device:TPU:12, one launch (start us, length us, event | category | flops | bytes accessed | tf_op | source)
XLA Modules:
  0.0 635.7 jit_solution(6201210966279950636)
XLA Ops:
  9.3 5.3 convolution_bitcast_fusion.1
  14.8 61.5 %all-gather.7.cloned.1.call-done = f32[16,4,8192]{2,1,0:T(4,128)} async-done(((f32[1,4,8192]{2,1,0:T(4,128)}), f32[16,4,8192]{2,1,0:T(4,128)}) %all-gather.7.cloned.1.call-update) | async-done | bytes 2097168 | tf_op jit(solution)/shard_map/all_gather | solution.py:12
  76.2 1.9 reduce_sum.92
  78.2 3.5 fusion.5
  82.4 1.9 copy.16
  84.3 71.3 %reduce-scatter.17.cloned.1.call-done = bf16[512,4]{1,0:T(8,128)(2,1)} async-done(((bf16[8192,4]{1,0:T(8,128)(2,1)}), bf16[512,4]{1,0:T(8,128)(2,1)}) %reduce-scatter.17.cloned.1.call-update) | async-done | bytes 4112
  156.6 2.5 psum.48
  159.1 4.6 convolution_convert_fusion.2
  163.6 1.9 copy.12
  166.4 77.7 %reduce-scatter.13.cloned.1.call-done = bf16[512,4]{1,0:T(8,128)(2,1)} async-done(((bf16[8192,4]{1,0:T(8,128)(2,1)}), bf16[512,4]{1,0:T(8,128)(2,1)}) %reduce-scatter.13.cloned.1.call-update) | async-done | bytes 4112
  244.1 1.7 multiply_reduce_fusion.2
  248.4 48.3 %all-reduce = (f32[]{:T(128)}, f32[]{:T(128)}) all-reduce(f32[]{:T(128)S(6)} %add.74, f32[]{:T(128)S(6)} %add.77), channel_id=1, replica_groups=mesh['grp'=2,'cores'=16] {'grp','cores'}, use_global_device_ids=true, to_apply=%region_2.3 | all-reduce | flops 2 | bytes 16 | tf_op jit(solution)/shard_map/psum | solution.py:54
  300.7 38.3 %psum.45 = f32[]{:T(128)} all-reduce(f32[]{:T(128)S(6)} %add.78), channel_id=1, replica_groups=mesh['grp'=2,'cores'=16] {'grp','cores'}, use_global_device_ids=true, to_apply=%region_12.13 | all-reduce | flops 1 | bytes 8 | tf_op jit(solution)/shard_map/psum | solution.py:54
  340.4 5.2 convolution_bitcast_fusion
  345.7 61.5 %all-gather.9.cloned.1.call-done = f32[16,4,8192]{2,1,0:T(4,128)} async-done(((f32[1,4,8192]{2,1,0:T(4,128)}), f32[16,4,8192]{2,1,0:T(4,128)}) %all-gather.9.cloned.1.call-update) | async-done | bytes 2097168 | tf_op jit(solution)/shard_map/all_gather | solution.py:12
  407.2 1.9 reduce_sum.97
  409.1 3.5 fusion.3
  413.3 1.9 copy.18
  415.3 71.3 %reduce-scatter.19.cloned.1.call-done = bf16[512,4]{1,0:T(8,128)(2,1)} async-done(((bf16[8192,4]{1,0:T(8,128)(2,1)}), bf16[512,4]{1,0:T(8,128)(2,1)}) %reduce-scatter.19.cloned.1.call-update) | async-done | bytes 4112
  487.5 2.5 psum.49
  490.0 4.6 convolution_convert_fusion
  494.6 1.9 copy.14
  497.2 77.8 %reduce-scatter.15.cloned.1.call-done = bf16[512,4]{1,0:T(8,128)(2,1)} async-done(((bf16[8192,4]{1,0:T(8,128)(2,1)}), bf16[512,4]{1,0:T(8,128)(2,1)}) %reduce-scatter.15.cloned.1.call-update) | async-done | bytes 4112
  578.0 48.3 %psum.47 = f32[]{:T(128)} all-reduce(f32[]{:T(128)S(6)} %add.83), channel_id=1, replica_groups=mesh['grp'=2,'cores'=16] {'grp','cores'}, use_global_device_ids=true, to_apply=%region_19.20 | all-reduce | flops 1 | bytes 8 | tf_op jit(solution)/shard_map/psum | solution.py:62
  (45 shorter events, 11.7 us)
Async XLA Ops:
  7.2 0.7 copy-start
  7.2 69.0 %all-gather.7.cloned.1.call-start = ((), (), s32[]{:S(2)}) async-start(), calls=%async_computation.4 | async-start | bytes 2228224 | tf_op jit(solution)/shard_map/all_gather | solution.py:12
  9.3 5.4 copy-start.5
  9.3 5.4 copy-start.6
  9.3 5.4 copy-start.7
  14.6 141.0 %reduce-scatter.17.cloned.1.call-start = ((), (), s32[]{:S(2)}) async-start(), calls=%async_computation.8 | async-start | bytes 2228224
  78.1 3.5 copy-start.1
  84.3 159.8 %reduce-scatter.13.cloned.1.call-start = ((), (), s32[]{:S(2)}) async-start(), calls=%async_computation.6 | async-start | bytes 2228224
  163.6 80.5 %copy-start.3 = (f32[4,512]{1,0:T(4,128)S(1)}, f32[4,512]{1,0:T(4,128)}, u32[]{:S(2)}) copy-start(f32[4,512]{1,0:T(4,128)} %param.10) | copy-start | bytes 24580
  163.6 80.5 %copy-start.4 = (f32[4,512]{1,0:T(4,128)S(1)}, f32[4,512]{1,0:T(4,128)}, u32[]{:S(2)}) copy-start(f32[4,512]{1,0:T(4,128)} %param.8) | copy-start | bytes 24580
  165.6 241.6 %all-gather.9.cloned.1.call-start = ((), (), s32[]{:S(2)}) async-start(), calls=%async_computation.5 | async-start | bytes 2228224 | tf_op jit(solution)/shard_map/all_gather | solution.py:12
  345.6 140.9 %reduce-scatter.19.cloned.1.call-start = ((), (), s32[]{:S(2)}) async-start(), calls=%async_computation.9 | async-start | bytes 2228224
  409.1 3.5 copy-start.2
  415.2 159.8 %reduce-scatter.15.cloned.1.call-start = ((), (), s32[]{:S(2)}) async-start(), calls=%async_computation.7 | async-start | bytes 2228224
Sparse Core Ops, SparseCore 0:
  14.7 61.4 all-gather.6
  84.4 71.1 reduce-scatter.16
  165.7 78.3 reduce-scatter.12
  345.7 61.3 all-gather.8
  415.3 71.1 reduce-scatter.18
  496.6 78.3 reduce-scatter.14
